TPU v7x, 1024 devices: a whole 4x8x16 slice. The times are simulated.
1024 devices in a mesh: dp: 16 (over y, core), expert: 64 (over z, x).
Axes of the slice: x: 4, y: 8, z: 16, core: 2. Of those that a mesh axis runs over, the one named last changes fastest.
Arguments:
- tokens: bfloat16 [4096, 7168], P('expert', 'dp'), may hold values from -6 to 6
- expert_ids: int32 [4096, 8], P('expert'), may hold values from 0 to 63, all different within a row; in each aligned block of 64 rows (0 to 63, 64 to 127, ...) at most 10 rows name the same one
- combine_weights: float32 [4096, 8], P('expert'), may hold values from 0.05 to 0.6
- w_gate: bfloat16 [64, 7168, 1024], P('expert', 'dp'), may hold values from -0.0625 to 0.0625
- w_up: bfloat16 [64, 7168, 1024], P('expert', 'dp'), may hold values from -0.0625 to 0.0625
- w_down: bfloat16 [64, 1024, 7168], P('expert', None, 'dp'), may hold values from -0.1875 to 0.1875
Outputs:
- combined: bfloat16 [4096, 7168], P('expert', 'dp')
Inputs may be any that keep to these rules, and one draw needn't show every extreme that they name: `expert_ids`: each row names 8 different experts. Within the rows of one device (aligned blocks of 64 rows) no expert is named by more than 10 rows, a bound that some block reaches.
All inputs are finite; a program needn't handle non-finite values.
Results may differ from a plain program's by a relative error of at most 0.0057.
Values may be sent and summed in bfloat16 or wider, within the bound.
A program may use at most 64 MiB of HBM per device.

v0:
```python
import jax
import jax.numpy as jnp
from jax import lax
from jax.sharding import PartitionSpec as P

CAP = 10


def shards(tokens, expert_ids, combine_weights, w_gate, w_up, w_down):
    tok_rows, width_part = tokens.shape
    top_count = expert_ids.shape[1]
    local_experts = w_gate.shape[0]
    owners = lax.axis_size("expert")
    experts = local_experts * owners
    expert_iota = lax.broadcasted_iota(jnp.int32, (1, 1, experts), 2)
    matches = (expert_ids[:, :, None] == expert_iota).astype(jnp.int32)
    per_token = jnp.sum(matches, axis=1)
    before = jnp.cumsum(per_token, axis=0) - per_token
    position = jnp.sum(matches * before[:, None, :], axis=2)
    slot_index = expert_ids * CAP + position
    slot_iota = lax.broadcasted_iota(jnp.int32, (experts * CAP, 1, 1), 0)
    placed = jnp.any(slot_index[None, :, :] == slot_iota, axis=2).astype(jnp.bfloat16)
    outgoing = jnp.dot(placed, tokens, preferred_element_type=jnp.float32).astype(jnp.bfloat16)
    incoming = lax.all_to_all(outgoing, "expert", split_axis=0, concat_axis=0, tiled=True)
    arrived = incoming.reshape(owners, local_experts, CAP, width_part)
    gate_part = jnp.einsum("hecd,edf->hecf", arrived, w_gate, preferred_element_type=jnp.float32)
    up_part = jnp.einsum("hecd,edf->hecf", arrived, w_up, preferred_element_type=jnp.float32)
    gate_sum, up_sum = (
        lax.psum_scatter(gate_part, "dp", scatter_dimension=3, tiled=True),
        lax.psum_scatter(up_part, "dp", scatter_dimension=3, tiled=True),
    )
    shares = (jax.nn.silu(gate_sum) * up_sum).astype(jnp.bfloat16)
    hidden = lax.all_gather(shares, "dp", axis=3, tiled=True)
    outputs = jnp.einsum(
        "hecf,efd->hecd", hidden, w_down, preferred_element_type=jnp.float32
    ).astype(jnp.bfloat16)
    returned = lax.all_to_all(
        outputs.reshape(owners * local_experts * CAP, width_part),
        "expert",
        split_axis=0,
        concat_axis=0,
        tiled=True,
    )
    picked = jnp.take(returned, slot_index.reshape(-1), axis=0).reshape(
        tok_rows, top_count, width_part
    )
    combined = jnp.sum(combine_weights[:, :, None] * picked.astype(jnp.float32), axis=1)
    return combined.astype(jnp.bfloat16)


def solution(mesh):
    placed = (
        P("expert", "dp"),
        P("expert", None),
        P("expert", None),
        P("expert", "dp", None),
        P("expert", "dp", None),
        P("expert", None, "dp"),
    )
    return jax.shard_map(
        shards, mesh=mesh, in_specs=placed, out_specs=P("expert", "dp"), check_vma=False
    )
```

profile of v0, /device:TPU:2, one launch (start us, length us, event | category | flops | bytes accessed | tf_op | source)
XLA Modules:
  0.0 376.6 jit_solution(11302064059883623087)
XLA Ops:
  6.5 0.0 copy-start
  6.5 0.0 reduce-scatter.7.cloned.1.call-start
  6.5 0.9 copy.42
  7.4 0.2 convert_reduce_fusion
  7.6 0.1 reduce_window_sum.11
  7.7 1.2 select_reduce_fusion
  8.9 0.1 copy.43
  9.0 0.7 compare_and_fusion
  9.7 0.1 copy.45
  9.8 0.0 copy-start.2
  9.8 0.6 copy-done.2
  10.4 0.5 fusion.1
  10.8 1.2 convolution_convert_fusion.1
  12.0 0.2 copy.46
  12.3 0.3 all_to_all.12
  12.6 77.3 %all_to_all.18 = bf16[64,10,448]{2,1,0:T(8,128)(2,1)S(1)} all-to-all(bf16[64,10,448]{2,1,0:T(8,128)(2,1)S(1)} %all_to_all.12), channel_id=1, replica_groups=mesh['dp'=16,'expert'=64] {'expert'}, dimensions={0} | all-to-all | bytes 1146880 | tf_op jit(solution)/shard_map/all_to_all | solution.py:24
  89.9 0.0 copy-start.1
  89.9 1.0 copy-done.1
  90.8 0.0 copy-done
  90.8 1.0 convolution_bitcast_fusion.1
  91.8 6.3 %copy.53 = f32[64,1,10,1024]{0,2,1,3:T(8,128)} copy(f32[64,1,10,1024]{3,0,2,1:T(8,128)S(1)} %convolution_bitcast_fusion.1) | data formatting | bytes 5242880
  98.1 7.1 %reshape.99 = f32[1024,640]{1,0:T(8,128)} reshape(f32[1024,1,10,64]{3,2,1,0:T(8,128)} %bitcast.40) | data formatting | bytes 5242880
  105.2 0.0 reduce-scatter.7.cloned.1.call-update
  105.3 0.0 reduce-scatter.9.cloned.1.call-start
  105.3 2.5 convolution_bitcast_fusion
  107.8 6.3 %copy.55 = f32[64,1,10,1024]{0,2,1,3:T(8,128)} copy(f32[64,1,10,1024]{3,0,2,1:T(8,128)S(1)} %convolution_bitcast_fusion) | data formatting | bytes 5242880
  114.1 7.2 %reshape.101 = f32[1024,640]{1,0:T(8,128)} reshape(f32[1024,1,10,64]{3,2,1,0:T(8,128)} %bitcast.41) | data formatting | bytes 5242880
  121.3 0.0 reduce-scatter.9.cloned.1.call-update
  121.3 0.0 all-gather.2.cloned.1.call-start
  121.3 43.9 %reduce-scatter.7.cloned.1.call-done = f32[64,640]{1,0:T(8,128)} async-done(((f32[1024,640]{1,0:T(8,128)}), f32[64,640]{1,0:T(8,128)}) %reduce-scatter.7.cloned.1.call-update) | async-done | bytes 163856
  165.2 1.0 reshape.100
  166.3 0.2 copy.54
  166.5 69.9 %reduce-scatter.9.cloned.1.call-done = f32[64,640]{1,0:T(8,128)} async-done(((f32[1024,640]{1,0:T(8,128)}), f32[64,640]{1,0:T(8,128)}) %reduce-scatter.9.cloned.1.call-update) | async-done | bytes 163856
  236.4 1.0 reshape.102
  237.4 0.2 copy.56
  237.6 0.1 multiply_convert_fusion
  237.7 0.9 copy.49
  238.7 0.0 all-gather.2.cloned.1.call-update
  238.7 0.0 copy-start.5
  238.7 49.4 %all-gather.2.cloned.1.call-done = bf16[64,1,10,1024]{0,2,1,3:T(8,128)(2,1)} async-done(((bf16[64,1,10,64]{0,2,1,3:T(8,128)(2,1)}), bf16[64,1,10,1024]{0,2,1,3:T(8,128)(2,1)}) %all-gather.2.cloned.1.call-update) | async-done | bytes 1310736 | tf_op jit(solution)/shard_map/all_gather | solution.py:33
  288.1 4.2 %copy.50 = bf16[64,1,10,1024]{3,0,2,1:T(8,128)(2,1)S(1)} copy(bf16[64,1,10,1024]{0,2,1,3:T(8,128)(2,1)} %all-gather.2.cloned.1.call-done) | data formatting | bytes 2621440 | tf_op jit(solution)/shard_map/all_gather | solution.py:33
  292.3 0.0 copy-done.5
  292.3 0.9 convolution_convert_fusion
  293.2 0.0 copy-start.3
  293.2 0.0 copy-start.4
  293.2 1.4 copy.51
  294.6 16.4 %all-to-all-start.1 = ((bf16[64,10,448]{2,1,0:T(8,128)(2,1)}), bf16[64,10,448]{2,1,0:T(8,128)(2,1)S(1)}, u32[]{:S(2)}, u32[]{:S(2)}) async-start(bf16[64,10,448]{2,1,0:T(8,128)(2,1)} %copy.51), calls=%async_computation.1 | async-start | bytes 2097152 | tf_op jit(solution)/shard_map/all_to_all | solution.py:37
  311.0 0.0 copy-done.3
  311.0 0.1 reshape.87
  311.1 0.1 copy.44
  311.2 0.0 copy-done.4
  311.2 0.1 copy.41
  311.3 55.3 %all-to-all-done.1 = bf16[64,10,448]{2,1,0:T(8,128)(2,1)S(1)} async-done(((bf16[64,10,448]{2,1,0:T(8,128)(2,1)}), bf16[64,10,448]{2,1,0:T(8,128)(2,1)S(1)}, u32[]{:S(2)}, u32[]{:S(2)}) %all-to-all-start.1) | async-done | bytes 573472 | tf_op jit(solution)/shard_map/all_to_all | solution.py:37
  366.6 0.4 all_to_all.15
  367.0 2.0 gather_fusion
  369.0 1.1 multiply_reduce_fusion
  (3 shorter events, 0.0 us)
Async XLA Ops:
  6.5 84.3 %copy-start = (bf16[1,448,1024]{2,1,0:T(8,128)(2,1)S(1)}, bf16[1,448,1024]{2,1,0:T(8,128)(2,1)}, u32[]{:S(2)}) copy-start(bf16[1,448,1024]{2,1,0:T(8,128)(2,1)} %param.9) | copy-start | bytes 2752516
  6.5 158.7 %reduce-scatter.7.cloned.1.call-start = ((), (), s32[]{:S(2)}) async-start(), calls=%async_computation.5 | async-start | bytes 2785280
  9.8 0.6 copy-start.2
  89.9 1.0 copy-start.1
  105.3 131.1 %reduce-scatter.9.cloned.1.call-start = ((), (), s32[]{:S(2)}) async-start(), calls=%async_computation.6 | async-start | bytes 2785280
  121.3 166.8 %all-gather.2.cloned.1.call-start = ((), (), s32[]{:S(2)}) async-start(), calls=%async_computation.4 | async-start | bytes 4456448 | tf_op jit(solution)/shard_map/all_gather | solution.py:33
  238.7 53.6 %copy-start.5 = (bf16[1,1024,448]{1,2,0:T(8,128)(2,1)S(1)}, bf16[1,1024,448]{1,2,0:T(8,128)(2,1)}, u32[]{:S(2)}) copy-start(bf16[1,1024,448]{1,2,0:T(8,128)(2,1)} %param.11) | copy-start | bytes 2752516
  293.2 17.9 %copy-start.3 = (s32[64,8]{1,0:T(8,128)S(1)}, s32[64,8]{1,0:T(8,128)}, u32[]{:S(2)}) copy-start(s32[64,8]{1,0:T(8,128)} %copy-done.2) | copy-start | bytes 6148
  293.2 18.1 %copy-start.4 = (f32[64,8]{0,1:T(8,128)S(1)}, f32[64,8]{0,1:T(8,128)}, u32[]{:S(2)}) copy-start(f32[64,8]{0,1:T(8,128)} %param.8) | copy-start | bytes 6148
  294.6 72.0 %all-to-all-start.1 = ((bf16[64,10,448]{2,1,0:T(8,128)(2,1)}), bf16[64,10,448]{2,1,0:T(8,128)(2,1)S(1)}, u32[]{:S(2)}, u32[]{:S(2)}) async-start(bf16[64,10,448]{2,1,0:T(8,128)(2,1)} %copy.51), calls=%async_computation.1 | async-start | bytes 2097152 | tf_op jit(solution)/shard_map/all_to_all | solution.py:37
Sparse Core Ops, SparseCore 0:
  105.4 59.7 reduce-scatter.6
  168.6 67.7 reduce-scatter.8
  239.1 48.9 all-gather.1
where the time goes:
time: 377 us
  waiting for transfers between devices  219 us (58%)
  blocking collectives  77.3 us (21%)
  local copies, waits for them, and re-layouts  41.6 us (11%)
  starting transfers between devices  16.5 us (4%)
  between operations  13.3 us (4%)
  matrix products  5.55 us (1%)
  other arithmetic  3.85 us (1%)
    unnamed x5, waiting for transfers between devices  114 us
    all_to_all x1, blocking collectives, shards(): lax.all_to_all(outgoing, 'expert', split_axis=0, concat_axis=0, tiled=True)  77.3 us
    all_to_all x1, waiting for transfers between devices, shards(): lax.all_to_all(outputs.reshape(owners * local_experts * CAP, width_part),...  55.3 us
    all_gather x1, waiting for transfers between devices, shards(): hidden = lax.all_gather(shares, 'dp', axis=3, tiled=True)  49.4 us
    unnamed x22, local copies, waits for them, and re-layouts  31.8 us
    all_to_all x1, starting transfers between devices, shards(): lax.all_to_all(outputs.reshape(owners * local_experts * CAP, width_part),...  16.4 us
  transfers between devices with their start and end apart: 4, of which 4 were waited for; matrix products, arithmetic and copies ran while one was open for 5% of the time, Pallas kernels for 0%

commit v1 on v0

v1 whole, which is shorter than its diff:
```python
import jax
import jax.numpy as jnp
from jax import lax
from jax.experimental import pallas as pl
from jax.experimental.pallas import tpu as pltpu
from jax.sharding import PartitionSpec as P

CAP = 10
NZ, NX, NY = 16, 4, 8
MESH = pl.DeviceIdType.MESH
F32, BF16 = jnp.float32, jnp.bfloat16


def place(sigma):
    return (sigma + 3) % NZ


def body(
    tok, ids, wts, wg_hbm, wu_hbm, wd_hbm, out,
    wg, wu, wd, blk, meta, xs, xr, wt_hi, wt_lo, part, prx, sb, rr, hid, ob, yb, pt, zs, rz,
    w_sem, own_sem, za_s, za_r, zm_s, zm_r, xa_s, xa_r, pp_s, pp_r, rs_s, rs_r,
    ag_s, ag_r, ph_s, ph_r, xb_s, xb_r, zr_s, zr_r,
):
    width = tok.shape[1]
    d, e = lax.axis_index("dp"), lax.axis_index("expert")
    y, c = d // 2, d % 2
    z, x = e // NX, e % NX

    z_dev = ({"expert": ((z + 1) % NZ) * NX + x}, {"expert": ((z + NZ - 1) % NZ) * NX + x})
    x_fwd = [None] + [{"expert": z * NX + (x + j) % NX} for j in range(1, NX)]
    x_bwd = [None] + [{"expert": z * NX + (x + NX - j) % NX} for j in range(1, NX)]
    y_dev = ({"dp": ((y + 1) % NY) * 2 + c}, {"dp": ((y + NY - 1) % NY) * 2 + c})
    partner = {"dp": y * 2 + (1 - c)}

    def remote(src, dst, ssem, rsem, dev):
        return pltpu.make_async_remote_copy(
            src_ref=src, dst_ref=dst, send_sem=ssem, recv_sem=rsem, device_id=dev, device_id_type=MESH
        )

    loads = [
        pltpu.make_async_copy(wg_hbm.at[0], wg, w_sem.at[0]),
        pltpu.make_async_copy(wu_hbm.at[0], wu, w_sem.at[1]),
        pltpu.make_async_copy(wd_hbm.at[0], wd, w_sem.at[2]),
    ]
    for load in loads:
        load.start()
    keep = pltpu.make_async_copy(tok, blk.at[place(0)], own_sem)
    keep.start()

    barrier = pltpu.get_barrier_semaphore()
    for dev in (*z_dev, *x_fwd[1:], *y_dev, partner):
        pl.semaphore_signal(barrier, inc=1, device_id=dev, device_id_type=MESH)

    e_iota = lax.broadcasted_iota(jnp.int32, (64, 64), 0)
    t_iota = lax.broadcasted_iota(jnp.int32, (64, 64), 1)
    named = jnp.zeros((64, 64), F32)
    for k in range(8):
        named = named + (e_iota == ids[k : k + 1, :]).astype(F32)
    before = jnp.dot(
        named.astype(BF16), (e_iota < t_iota).astype(F32).astype(BF16), preferred_element_type=F32
    )
    for k in range(8):
        row = ids[k : k + 1, :]
        position = jnp.sum(jnp.where(e_iota == row, before, 0.0), axis=0, keepdims=True)
        meta[place(0), k : k + 1, 0:64] = row.astype(F32) * 16.0 + position
    meta[place(0), :, 64:128] = wts[...]

    pl.semaphore_wait(barrier, 8)

    def ring_place(way, k):
        return place(k if way == 0 else (NZ - k) % NZ)

    half = 32
    za, zm = {}, {}
    for way in range(2):
        for k in range(1, 9):
            for sub in range(2):
                if k == 8 and sub != way:
                    continue
                rows = pl.ds(sub * half, half)
                src = tok.at[rows] if k == 1 else blk.at[ring_place(way, k - 1), rows]
                za[way, k, sub] = remote(
                    src, blk.at[ring_place(way, k), rows], za_s.at[way, k - 1, sub], za_r.at[way, k - 1, sub], z_dev[way]
                )
            if k < 8 or way == 0:
                zm[way, k] = remote(
                    meta.at[ring_place(way, k - 1)], meta.at[ring_place(way, k)],
                    zm_s.at[way, k - 1], zm_r.at[way, k - 1], z_dev[way],
                )

    def z_step(k):
        for sub in range(2):
            for way in range(2):
                if sub == 0:
                    if k > 1:
                        zm[way, k - 1].wait_recv()
                    if (way, k) in zm:
                        zm[way, k].start()
                if k > 1:
                    za[way, k - 1, sub].wait_recv()
                if (way, k, sub) in za:
                    za[way, k, sub].start()

    lane = lax.broadcasted_iota(jnp.int32, (8, 128), 1)
    row_iota = lax.broadcasted_iota(jnp.int32, (80, 512), 0).astype(F32)
    src_row = (lax.broadcasted_iota(jnp.int32, (1, 512), 1) // 64 * CAP).astype(F32)
    xa = {}
    for g in range(2):
        for j in range(1, NX):
            xa[g, j] = remote(xs.at[g, j - 1], xr.at[g, j], xa_s.at[g, j - 1], xa_r.at[g, j - 1], x_fwd[j])

    def select(g):
        codes, weights = [], []
        for s in range(0, 8, 2):
            a, b = meta[8 * g + s], meta[8 * g + s + 1]
            codes.append(jnp.where(lane < 64, a, pltpu.roll(b, 64, 1)))
            weights.append(jnp.where(lane < 64, pltpu.roll(a, 64, 1), b))
        code = jnp.concatenate(codes, axis=1)
        weight = jnp.concatenate(weights, axis=1)
        rows = blk[8 * g : 8 * g + 8].reshape(512, width)
        for j in (2, 1, 3, 0):
            base = ((z * NX + (x + j) % NX) * 16).astype(F32)
            own = code - base
            hit = jnp.logical_and(own >= 0.0, own < 16.0)
            slot = jnp.max(jnp.where(hit, own, -1.0), axis=0, keepdims=True)
            share = jnp.sum(jnp.where(hit, weight, 0.0), axis=0, keepdims=True)
            target = jnp.where(slot >= 0.0, slot + src_row, -1.0)
            chosen = row_iota == target
            pick = jnp.dot(chosen.astype(F32).astype(BF16), rows, preferred_element_type=F32).astype(BF16)
            if j:
                xs[g, j - 1] = pick
                xa[g, j].start()
            else:
                xr[g, 0] = pick
            scaled = jnp.where(chosen, share, 0.0)
            high = scaled.astype(BF16)
            wt_hi[g, 80 * j : 80 * j + 80, :] = high
            wt_lo[g, 80 * j : 80 * j + 80, :] = (scaled - high.astype(F32)).astype(BF16)

    def pair(g, s):
        return remote(part.at[g, s, 1 - c], prx.at[g, s], pp_s.at[g, s], pp_r.at[g, s], partner)

    def parts(g):
        rows = xr[g].reshape(320, width)

        def piece(s, carry):
            at_g = pl.multiple_of((y + 2 * NY - 1 - s) % NY * 128, 128)
            at_u = pl.multiple_of((y + 1 + s) % NY * 128, 128)
            gate = jnp.dot(rows, wg[:, pl.ds(at_g, 128)], preferred_element_type=F32)
            up = jnp.dot(rows, wu[:, pl.ds(at_u, 128)], preferred_element_type=F32)
            part[g, s, :, 0] = gate.reshape(2, 160, 128)
            part[g, s, :, 1] = up.reshape(2, 160, 128)
            pair(g, s).start()
            return carry

        lax.fori_loop(0, NY, piece, 0)

    rs = {}
    for g in range(2):
        for s in range(NY - 1):
            for m in range(2):
                rs[g, s, m] = remote(sb.at[g, s, m], rr.at[g, s, m], rs_s.at[g, s, m], rs_r.at[g, s, m], y_dev[m])

    def y_step(g, s):
        pair(g, s).wait_recv()
        for m in range(2):
            value = part[g, s, c, m] + prx[g, s, m]
            if s:
                rs[g, s - 1, m].wait_recv()
                value = value + rr[g, s - 1, m]
            sb[g, s, m] = value
            rs[g, s, m].start()

    def unit(k):
        return pl.ds(pl.multiple_of((y + 2 * NY - k) % NY * 128, 128), 128)

    ag, ph = {}, {}
    for g in range(2):
        for way in range(2):
            last = 4 if way == g else 3
            for k in range(1, last + 1):
                near = unit(k - 1 if way == 0 else 1 - k)
                there = hid.at[g, c, :, near]
                ag[g, way, k] = remote(there, there, ag_s.at[g, way, k - 1], ag_r.at[g, way, k - 1], y_dev[way])
        for sigma in range(-4, 5):
            ph[g, sigma] = None

    def hand(g, index, sigma):
        there = hid.at[g, c, :, unit(sigma)]
        return remote(there, hid.at[g, c, :, unit(sigma)], ph_s.at[g, index], ph_r.at[g, index], partner)

    def received(g, index, sigma):
        there = hid.at[g, 1 - c, :, unit(sigma)]
        return remote(there, there, ph_s.at[g, index], ph_r.at[g, index], partner)

    def arrived(g, way, k):
        there = hid.at[g, c, :, unit(k if way == 0 else -k)]
        return remote(there, there, ag_s.at[g, way, k - 1], ag_r.at[g, way, k - 1], y_dev[way])

    def activate(g):
        pair(g, NY - 1).wait_recv()
        for m in range(2):
            rs[g, NY - 2, m].wait_recv()
        gate = part[g, NY - 1, c, 0] + prx[g, NY - 1, 0] + rr[g, NY - 2, 0]
        up = part[g, NY - 1, c, 1] + prx[g, NY - 1, 1] + rr[g, NY - 2, 1]
        hid[g, c, :, unit(0)] = (gate / (1.0 + jnp.exp(-gate)) * up).astype(BF16)
        for way in range(2):
            ag[g, way, 1].start()
        hand(g, 0, 0).start()

    order = {g: [0] for g in range(2)}

    def gather_step(g, k):
        for way in range(2):
            if (g, way, k) not in ag:
                continue
            arrived(g, way, k).wait_recv()
            if (g, way, k + 1) in ag:
                ag[g, way, k + 1].start()
            sigma = k if way == 0 else -k
            hand(g, len(order[g]), sigma).start()
            order[g].append(sigma)

    xb = {}
    for g in range(2):
        for j in range(1, NX):
            xb[g, j] = remote(ob.at[g, j], yb.at[g, j], xb_s.at[g, j - 1], xb_r.at[g, j - 1], x_bwd[j])

    def down(g):
        for index, sigma in enumerate(order[g]):
            received(g, index, sigma).wait_recv()
        for h in (1, 0):
            res = jnp.dot(hid[g, h], wd[...], preferred_element_type=F32).astype(BF16).reshape(2, 80, width)
            if h:
                ob[g, 2] = res[0]
                xb[g, 2].start()
                ob[g, 3] = res[1]
                xb[g, 3].start()
            else:
                ob[g, 1] = res[1]
                xb[g, 1].start()
                yb[g, 0] = res[0]

    def combine(g):
        for j in range(1, NX):
            xb[g, j].wait_recv()
        rows = yb[g].reshape(320, width)
        dims = (((0,), (0,)), ((), ()))
        res = lax.dot_general(wt_hi[g], rows, dims, preferred_element_type=F32)
        res = res + lax.dot_general(wt_lo[g], rows, dims, preferred_element_type=F32)
        pt[8 * g : 8 * g + 8] = res.reshape(8, 64, width)

    zr = {}
    for way in range(2):
        for k in range(1, 9):
            for sub in range(2):
                if k == 8 and sub != way:
                    continue
                zr[way, k, sub] = remote(
                    zs.at[way, k - 1, sub], rz.at[way, k - 1, sub], zr_s.at[way, k - 1, sub], zr_r.at[way, k - 1, sub], z_dev[way]
                )

    def z_sum(k):
        for sub in range(2):
            for way in range(2):
                if (way, k, sub) not in zr:
                    continue
                at = ring_place(1 - way, k)
                value = pt[at, sub * half : (sub + 1) * half, :]
                if (way, k + 1, sub) in zr:
                    zr[way, k + 1, sub].wait_recv()
                    value = value + rz[way, k, sub].astype(F32)
                zs[way, k - 1, sub] = value.astype(BF16)
                zr[way, k, sub].start()

    for k in range(1, 6):
        z_step(k)
    keep.wait()
    select(0)
    for k in range(6, 9):
        z_step(k)
    za[0, 8, 0].wait_recv()
    za[1, 8, 1].wait_recv()
    zm[0, 8].wait_recv()
    select(1)
    loads[0].wait()
    loads[1].wait()
    for g in range(2):
        for j in range(1, NX):
            xa[g, j].wait_recv()
        parts(g)
        if g == 0:
            y_step(0, 0)
    for s in range(NY - 1):
        if s:
            y_step(0, s)
        y_step(1, s)
    activate(0)
    activate(1)
    for k in range(1, 5):
        gather_step(0, k)
        gather_step(1, k)
    loads[2].wait()
    down(0)
    down(1)
    combine(1)
    for k in range(8, 4, -1):
        z_sum(k)
    combine(0)
    for k in range(4, 0, -1):
        z_sum(k)
    for sub in range(2):
        total = pt[place(0), sub * half : (sub + 1) * half, :]
        for way in range(2):
            zr[way, 1, sub].wait_recv()
            total = total + rz[way, 0, sub].astype(F32)
        out[sub * half : (sub + 1) * half, :] = total.astype(BF16)

    for copies in (za, zm, xa, rs, ag, xb, zr):
        for copy in copies.values():
            copy.wait_send()
    for g in range(2):
        for s in range(NY):
            pair(g, s).wait_send()
        for index, sigma in enumerate(order[g]):
            hand(g, index, sigma).wait_send()


def shards(tokens, expert_ids, combine_weights, w_gate, w_up, w_down):
    rows, width = tokens.shape
    hidden = w_gate.shape[2]
    vmem = pl.BlockSpec(memory_space=pltpu.VMEM)
    hbm = pl.BlockSpec(memory_space=pl.ANY)
    dma = pltpu.SemaphoreType.DMA
    return pl.pallas_call(
        body,
        out_shape=jax.ShapeDtypeStruct((rows, width), BF16),
        in_specs=[vmem, vmem, vmem, hbm, hbm, hbm],
        out_specs=vmem,
        scratch_shapes=[
            pltpu.VMEM((width, hidden), BF16),
            pltpu.VMEM((width, hidden), BF16),
            pltpu.VMEM((hidden, width), BF16),
            pltpu.VMEM((16, 64, width), BF16),
            pltpu.VMEM((16, 8, 128), F32),
            pltpu.VMEM((2, 3, 80, width), BF16),
            pltpu.VMEM((2, 4, 80, width), BF16),
            pltpu.VMEM((2, 320, 512), BF16),
            pltpu.VMEM((2, 320, 512), BF16),
            pltpu.VMEM((2, 8, 2, 2, 160, 128), F32),
            pltpu.VMEM((2, 8, 2, 160, 128), F32),
            pltpu.VMEM((2, 7, 2, 160, 128), F32),
            pltpu.VMEM((2, 7, 2, 160, 128), F32),
            pltpu.VMEM((2, 2, 160, hidden), BF16),
            pltpu.VMEM((2, 4, 80, width), BF16),
            pltpu.VMEM((2, 4, 80, width), BF16),
            pltpu.VMEM((16, 64, width), F32),
            pltpu.VMEM((2, 8, 2, 32, width), BF16),
            pltpu.VMEM((2, 8, 2, 32, width), BF16),
            dma((3,)),
            dma,
            dma((2, 8, 2)),
            dma((2, 8, 2)),
            dma((2, 8)),
            dma((2, 8)),
            dma((2, 3)),
            dma((2, 3)),
            dma((2, 8)),
            dma((2, 8)),
            dma((2, 7, 2)),
            dma((2, 7, 2)),
            dma((2, 2, 4)),
            dma((2, 2, 4)),
            dma((2, 8)),
            dma((2, 8)),
            dma((2, 3)),
            dma((2, 3)),
            dma((2, 8, 2)),
            dma((2, 8, 2)),
        ],
        compiler_params=pltpu.CompilerParams(
            collective_id=0, has_side_effects=True, vmem_limit_bytes=60 * 1024 * 1024
        ),
    )(tokens, expert_ids.T, combine_weights.T, w_gate, w_up, w_down)


def solution(mesh):
    placed = (
        P("expert", "dp"),
        P("expert", None),
        P("expert", None),
        P("expert", "dp", None),
        P("expert", "dp", None),
        P("expert", None, "dp"),
    )
    return jax.shard_map(
        shards, mesh=mesh, in_specs=placed, out_specs=P("expert", "dp"), check_vma=False
    )
```

time: 377 us -> 142 us (0.38)
  the two profiles are of different devices: /device:TPU:2 before, /device:TPU:64 now
where the time goes in v1:
time: 142 us; the launch traced here: 141 us
  Pallas kernels  138 us (97%)
  local copies, waits for them, and re-layouts  3.73 us (3%)
    pallas_call x1, Pallas kernels, shards(): pl.pallas_call(body, out_shape=jax.ShapeDtypeStruct((rows, width), BF16),...  138 us
    unnamed x2, local copies, waits for them, and re-layouts  3.73 us

profile of v1, /device:TPU:64, one launch (start us, length us, event | category | flops | bytes accessed | tf_op | source)
XLA Modules:
  0.0 141.3 jit_solution(18010663858498527452)
XLA Ops:
  0.0 2.3 %copy.7.wd_hbm = bf16[1,1024,448]{2,1,0:T(8,128)(2,1)} copy(bf16[1,1024,448]{1,2,0:T(8,128)(2,1)} %param.11) | data formatting | bytes 1835008 | tf_op args[5]
  2.3 137.6 %shard_map.64 = bf16[64,448]{1,0:T(8,128)(2,1)} custom-call(bf16[64,448]{1,0:T(8,128)(2,1)} %tok.1, s32[8,64]{1,0:T(8,128)} %bitcast.2, f32[8,64]{1,0:T(8,128)} %bitcast.3, bf16[1,448,1024]{2,1,0:T(8,128)(2,1)} %wg_hbm.1, bf16[1,448,1024]{2,1,0:T(8,128)(2,1)} %wu_hbm.1, bf16[1,1024,448]{2,1,0:T(8,128)(2,1)} %copy.7.wd_hbm), custom_call_target="tpu_custom_call" | custom-call | tf_op jit(solution)/shard_map/pallas_call | solution.py:335
  139.9 1.5 %copy.9 = bf16[64,448]{1,0:T(8,128)(2,1)} copy(bf16[64,448]{1,0:T(8,128)(2,1)} %shard_map.64) | data formatting | bytes 114688

commit v2 on v1

v2 whole, which is shorter than its diff:
```python
import jax
import jax.numpy as jnp
from jax import lax
from jax.experimental import pallas as pl
from jax.experimental.pallas import tpu as pltpu
from jax.sharding import PartitionSpec as P

CAP = 10
NZ, NX, NY, NS = 16, 4, 8, 2
MESH = pl.DeviceIdType.MESH
F32, BF16 = jnp.float32, jnp.bfloat16


def place(sigma):
    return (sigma + 3) % NZ


def body(
    tok, ids, wts, wg_hbm, wu_hbm, wd_hbm, out,
    wg, wu, wd, blk, meta, xs, xr, wt_hi, wt_lo, part, prx, sb, rr, hid, ob, yb, pt, zs, rz,
    w_sem, za_s, za_r, zm_s, zm_r, xa_s, xa_r, pp_s, pp_r, rs_s, rs_r,
    ag_s, ag_r, ph_s, ph_r, xb_s, xb_r, zr_s, zr_r,
):
    width, padded = tok.shape[1], blk.shape[2]
    d, e = lax.axis_index("dp"), lax.axis_index("expert")
    y, c = d // 2, d % 2
    z, x = e // NX, e % NX

    z_dev = ({"expert": ((z + 1) % NZ) * NX + x}, {"expert": ((z + NZ - 1) % NZ) * NX + x})
    z_two = ({"expert": ((z + 2) % NZ) * NX + x}, {"expert": ((z + NZ - 2) % NZ) * NX + x})
    x_fwd = [None] + [{"expert": z * NX + (x + j) % NX} for j in range(1, NX)]
    x_bwd = [None] + [{"expert": z * NX + (x + NX - j) % NX} for j in range(1, NX)]
    y_dev = ({"dp": ((y + 1) % NY) * 2 + c}, {"dp": ((y + NY - 1) % NY) * 2 + c})
    y_two = ({"dp": ((y + 2) % NY) * 2 + c}, {"dp": ((y + NY - 2) % NY) * 2 + c})
    partner = {"dp": y * 2 + (1 - c)}

    def remote(src, dst, ssem, rsem, dev):
        return pltpu.make_async_remote_copy(
            src_ref=src, dst_ref=dst, send_sem=ssem, recv_sem=rsem, device_id=dev, device_id_type=MESH
        )

    loads = [
        pltpu.make_async_copy(wg_hbm.at[0], wg.at[pl.ds(0, width)], w_sem.at[0]),
        pltpu.make_async_copy(wu_hbm.at[0], wu.at[pl.ds(0, width)], w_sem.at[1]),
        pltpu.make_async_copy(wd_hbm.at[0], wd.at[pl.ds(0, width)], w_sem.at[2]),
    ]
    for load in loads:
        load.start()
    barrier = pltpu.get_barrier_semaphore()
    for dev in (*z_dev, *z_two, *x_fwd[1:], *y_dev, *y_two, partner):
        pl.semaphore_signal(barrier, inc=1, device_id=dev, device_id_type=MESH)

    def routing():
        e_iota = lax.broadcasted_iota(jnp.int32, (64, 64), 0)
        t_iota = lax.broadcasted_iota(jnp.int32, (64, 64), 1)
        named = jnp.zeros((64, 64), F32)
        for k in range(8):
            named = named + (e_iota == ids[k : k + 1, :]).astype(F32)
        before = jnp.dot(
            named.astype(BF16), (e_iota < t_iota).astype(F32).astype(BF16), preferred_element_type=F32
        )
        for k in range(8):
            row = ids[k : k + 1, :]
            position = jnp.sum(jnp.where(e_iota == row, before, 0.0), axis=0, keepdims=True)
            meta[place(0), k : k + 1, 0:64] = row.astype(F32) * 16.0 + position
        meta[place(0), :, 64:128] = wts[...]

    blk[place(0)] = jnp.zeros((64, padded), BF16)
    blk[place(0), :, 0:width] = tok[...]
    for weight in (wg, wu, wd):
        weight[width:padded, :] = jnp.zeros((padded - width, weight.shape[1]), BF16)
    pl.semaphore_wait(barrier, 12)

    def ring_place(way, k):
        return place(k if way == 0 else (NZ - k) % NZ)

    half = 64 // NS
    za, zm = {}, {}
    for way in range(2):
        for k in range(1, 9):
            for sub in range(NS):
                if k == 8 and sub * 2 // NS != way:
                    continue
                rows = pl.ds(sub * half, half)
                src = blk.at[ring_place(way, (k - 1) // 2 * 2), rows]
                za[way, k, sub] = remote(
                    src, blk.at[ring_place(way, k), rows], za_s.at[way, k - 1, sub], za_r.at[way, k - 1, sub],
                    (z_dev if k % 2 else z_two)[way],
                )
            if k < 8 or way == 0:
                zm[way, k] = remote(
                    meta.at[ring_place(way, (k - 1) // 2 * 2)], meta.at[ring_place(way, k)],
                    zm_s.at[way, k - 1], zm_r.at[way, k - 1], (z_dev if k % 2 else z_two)[way],
                )

    def z_go(k):
        for sub in range(NS):
            for way in range(2):
                if k:
                    za[way, k, sub].wait_recv()
                for onward in (k + 2, k + 1):
                    if (way, onward, sub) in za:
                        za[way, onward, sub].start()
        if k == 0:
            routing()
        for way in range(2):
            if k:
                zm[way, k].wait_recv()
            for onward in (k + 2, k + 1):
                if (way, onward) in zm:
                    zm[way, onward].start()

    def z_take(*ks):
        for k in ks:
            for way in range(2):
                for sub in range(NS):
                    if (way, k, sub) in za:
                        za[way, k, sub].wait_recv()
                if (way, k) in zm:
                    zm[way, k].wait_recv()

    lane = lax.broadcasted_iota(jnp.int32, (8, 128), 1)
    row_iota = lax.broadcasted_iota(jnp.int32, (80, 512), 0).astype(F32)
    src_row = (lax.broadcasted_iota(jnp.int32, (1, 512), 1) // 64 * CAP).astype(F32)
    xa = {}
    for g in range(2):
        for j in range(1, NX):
            xa[g, j] = remote(xs.at[g, j - 1], xr.at[g, j], xa_s.at[g, j - 1], xa_r.at[g, j - 1], x_fwd[j])

    def select(g):
        codes, weights = [], []
        for s in range(0, 8, 2):
            a, b = meta[8 * g + s], meta[8 * g + s + 1]
            codes.append(jnp.where(lane < 64, a, pltpu.roll(b, 64, 1)))
            weights.append(jnp.where(lane < 64, pltpu.roll(a, 64, 1), b))
        code = jnp.concatenate(codes, axis=1)
        weight = jnp.concatenate(weights, axis=1)
        rows = blk[8 * g : 8 * g + 8].reshape(512, padded)
        for j in (2, 1, 3, 0):
            base = ((z * NX + (x + j) % NX) * 16).astype(F32)
            own = code - base
            hit = jnp.logical_and(own >= 0.0, own < 16.0)
            slot = jnp.max(jnp.where(hit, own, -1.0), axis=0, keepdims=True)
            share = jnp.sum(jnp.where(hit, weight, 0.0), axis=0, keepdims=True)
            target = jnp.where(slot >= 0.0, slot + src_row, -1.0)
            chosen = row_iota == target
            pick = jnp.dot(chosen.astype(F32).astype(BF16), rows, preferred_element_type=F32).astype(BF16)
            if j:
                xs[g, j - 1] = pick
                xa[g, j].start()
            else:
                xr[g, 0] = pick
            scaled = jnp.where(chosen, share, 0.0)
            high = scaled.astype(BF16)
            wt_hi[g, 80 * j : 80 * j + 80, :] = high
            wt_lo[g, 80 * j : 80 * j + 80, :] = (scaled - high.astype(F32)).astype(BF16)

    def pair(g, s):
        return remote(part.at[g, s, 1 - c], prx.at[g, s], pp_s.at[g, s], pp_r.at[g, s], partner)

    def parts(g, low, high):
        rows = xr[g].reshape(320, padded)

        def piece(s, carry):
            offset = (4 - (s + 1) // 2) * (2 * (s % 2) - 1)
            at = pl.multiple_of((y + NY + offset) % NY * 128, 128)
            gate = jnp.dot(rows, wg[:, pl.ds(at, 128)], preferred_element_type=F32)
            up = jnp.dot(rows, wu[:, pl.ds(at, 128)], preferred_element_type=F32)
            part[g, s, :, 0] = gate.reshape(2, 160, 128)
            part[g, s, :, 1] = up.reshape(2, 160, 128)
            pair(g, s).start()
            return carry

        lax.fori_loop(low, high, piece, 0)

    rs = {}
    for g in range(2):
        for way in range(2):
            for k in range(1, 5):
                for m in range(2):
                    if k == 4 and m != way:
                        continue
                    rs[g, way, k, m] = remote(
                        sb.at[g, way, k - 1, m], rr.at[g, way, k - 1, m],
                        rs_s.at[g, way, k - 1, m], rs_r.at[g, way, k - 1, m], y_dev[way],
                    )

    def y_step(g, k):
        for s in (0,) if k == 4 else (7 - 2 * k, 8 - 2 * k):
            pair(g, s).wait_recv()
        for m in range(2):
            for way in range(2):
                if (g, way, k, m) not in rs:
                    continue
                s = 0 if k == 4 else 7 - 2 * k + way
                value = part[g, s, c, m] + prx[g, s, m]
                if (g, way, k + 1, m) in rs:
                    rs[g, way, k + 1, m].wait_recv()
                    value = value + rr[g, way, k, m]
                sb[g, way, k - 1, m] = value
                rs[g, way, k, m].start()

    def unit(k):
        return (y + 2 * NY - k) % NY

    ag, order = {}, {}
    for g in range(2):
        for way in range(2):
            sign = 1 if way == 0 else -1
            for near in range(1, 5):
                if near == 4 and way != g:
                    continue
                held = hid.at[g, c, unit(0 if near < 3 else 2 * sign)]
                ag[g, sign * near] = remote(
                    held, held, ag_s.at[g, sign * near + 4], ag_r.at[g, sign * near + 4],
                    (y_dev if near % 2 else y_two)[way],
                )
        order[g] = [0, 1, -1, 2, -2, 3, -3, 4 if g == 0 else -4]

    def arrived(g, sigma):
        there = hid.at[g, c, unit(sigma)]
        dev = y_dev[0 if sigma > 0 else 1]
        return remote(there, there, ag_s.at[g, sigma + 4], ag_r.at[g, sigma + 4], dev)

    def hand(g, index, sigma):
        there = hid.at[g, c, unit(sigma)]
        return remote(there, there, ph_s.at[g, index], ph_r.at[g, index], partner)

    def received(g, index, sigma):
        there = hid.at[g, 1 - c, unit(sigma)]
        return remote(there, there, ph_s.at[g, index], ph_r.at[g, index], partner)

    def activate(g):
        pair(g, NY - 1).wait_recv()
        sums = []
        for m in range(2):
            value = part[g, NY - 1, c, m] + prx[g, NY - 1, m]
            for way in range(2):
                rs[g, way, 1, m].wait_recv()
                value = value + rr[g, way, 0, m]
            sums.append(value)
        gate, up = sums
        hid[g, c, unit(0)] = (gate / (1.0 + jnp.exp(-gate)) * up).astype(BF16)
        for sigma in (2, -2, 1, -1):
            ag[g, sigma].start()
        hand(g, 0, 0).start()

    def gather(g, low, high):
        for index in range(low, high):
            sigma = order[g][index]
            arrived(g, sigma).wait_recv()
            if abs(sigma) == 2:
                for onward in (sigma * 2, sigma * 3 // 2):
                    if (g, onward) in ag:
                        ag[g, onward].start()
            hand(g, index, sigma).start()

    xb = {}
    for g in range(2):
        for j in range(1, NX):
            xb[g, j] = remote(ob.at[g, j], yb.at[g, j], xb_s.at[g, j - 1], xb_r.at[g, j - 1], x_bwd[j])

    def down(g):
        for index, sigma in enumerate(order[g]):
            received(g, index, sigma).wait_recv()
        for h in (1, 0):
            rows = jnp.concatenate([hid[g, h, u] for u in range(NY)], axis=1)
            res = lax.dot_general(rows, wd[...], (((1,), (1,)), ((), ())), preferred_element_type=F32)
            res = res.astype(BF16).reshape(2, 80, padded)
            if h:
                ob[g, 2] = res[0]
                xb[g, 2].start()
                ob[g, 3] = res[1]
                xb[g, 3].start()
            else:
                ob[g, 1] = res[1]
                xb[g, 1].start()
                yb[g, 0] = res[0]

    def combine(g):
        for j in range(1, NX):
            xb[g, j].wait_recv()
        rows = yb[g].reshape(320, padded)
        dims = (((0,), (0,)), ((), ()))
        res = lax.dot_general(wt_hi[g], rows, dims, preferred_element_type=F32)
        res = res + lax.dot_general(wt_lo[g], rows, dims, preferred_element_type=F32)
        pt[8 * g : 8 * g + 8] = res.reshape(8, 64, padded)

    zr = {}
    for way in range(2):
        for k in range(1, 9):
            for sub in range(NS):
                if k == 8 and sub * 2 // NS != way:
                    continue
                zr[way, k, sub] = remote(
                    zs.at[way, k - 1, sub], rz.at[way, k - 1, sub], zr_s.at[way, k - 1, sub], zr_r.at[way, k - 1, sub],
                    (z_dev if k % 2 else z_two)[way],
                )

    def z_sum(k):
        for sub in range(NS):
            for way in range(2):
                if (way, k, sub) not in zr:
                    continue
                at = ring_place(1 - way, k)
                value = pt[at, sub * half : (sub + 1) * half, :]
                for before in (k + 1, k + 2):
                    if k % 2 == 0 and (way, before, sub) in zr:
                        zr[way, before, sub].wait_recv()
                        value = value + rz[way, before - 1, sub].astype(F32)
                zs[way, k - 1, sub] = value.astype(BF16)
                zr[way, k, sub].start()

    def sent(*groups):
        for copies in groups:
            for copy in copies:
                copy.wait_send()

    z_go(0)
    z_go(2)
    z_go(4)
    z_take(1, 3)
    select(0)
    loads[0].wait()
    loads[1].wait()
    for j in range(1, NX):
        xa[0, j].wait_recv()
    parts(0, 0, 3)
    z_go(6)
    y_step(0, 4)
    parts(0, 3, 5)
    y_step(0, 3)
    parts(0, 5, 8)
    z_take(5, 7, 8)
    select(1)
    y_step(0, 2)
    for j in range(1, NX):
        xa[1, j].wait_recv()
    parts(1, 0, 3)
    y_step(1, 4)
    y_step(0, 1)
    parts(1, 3, 5)
    y_step(1, 3)
    activate(0)
    parts(1, 5, 8)
    y_step(1, 2)
    gather(0, 1, 5)
    y_step(1, 1)
    gather(0, 5, 8)
    activate(1)
    loads[2].wait()
    down(0)
    sent(za.values(), zm.values(), xa.values())
    gather(1, 1, 5)
    sent(pair(g, s) for g in range(2) for s in range(NY))
    gather(1, 5, 8)
    down(1)
    combine(0)
    z_sum(3)
    z_sum(1)
    sent(rs.values(), ag.values())
    sent(hand(g, index, sigma) for g in range(2) for index, sigma in enumerate(order[g]))
    combine(1)
    for k in (8, 7, 5, 6, 4, 2):
        z_sum(k)
    sent(xb.values())
    for sub in range(NS):
        total = pt[place(0), sub * half : (sub + 1) * half, :]
        for way in range(2):
            for k in (1, 2):
                zr[way, k, sub].wait_recv()
                total = total + rz[way, k - 1, sub].astype(F32)
        out[sub * half : (sub + 1) * half, :] = total[:, 0:width].astype(BF16)
    sent(zr.values())


def shards(tokens, expert_ids, combine_weights, w_gate, w_up, w_down):
    rows, width = tokens.shape
    padded = pl.cdiv(width, 128) * 128
    hidden = w_gate.shape[2]
    vmem = pl.BlockSpec(memory_space=pltpu.VMEM)
    hbm = pl.BlockSpec(memory_space=pl.ANY)
    dma = pltpu.SemaphoreType.DMA
    return pl.pallas_call(
        body,
        out_shape=jax.ShapeDtypeStruct((rows, width), BF16),
        in_specs=[vmem, vmem, vmem, hbm, hbm, hbm],
        out_specs=vmem,
        scratch_shapes=[
            pltpu.VMEM((padded, hidden), BF16),
            pltpu.VMEM((padded, hidden), BF16),
            pltpu.VMEM((padded, hidden), BF16),
            pltpu.VMEM((16, 64, padded), BF16),
            pltpu.VMEM((16, 8, 128), F32),
            pltpu.VMEM((2, 3, 80, padded), BF16),
            pltpu.VMEM((2, 4, 80, padded), BF16),
            pltpu.VMEM((2, 320, 512), BF16),
            pltpu.VMEM((2, 320, 512), BF16),
            pltpu.VMEM((2, 8, 2, 2, 160, 128), F32),
            pltpu.VMEM((2, 8, 2, 160, 128), F32),
            pltpu.VMEM((2, 2, 4, 2, 160, 128), F32),
            pltpu.VMEM((2, 2, 4, 2, 160, 128), F32),
            pltpu.VMEM((2, 2, 8, 160, 128), BF16),
            pltpu.VMEM((2, 4, 80, padded), BF16),
            pltpu.VMEM((2, 4, 80, padded), BF16),
            pltpu.VMEM((16, 64, padded), F32),
            pltpu.VMEM((2, 8, NS, 64 // NS, padded), BF16),
            pltpu.VMEM((2, 8, NS, 64 // NS, padded), BF16),
            dma((3,)),
            dma((2, 8, NS)),
            dma((2, 8, NS)),
            dma((2, 8)),
            dma((2, 8)),
            dma((2, 3)),
            dma((2, 3)),
            dma((2, 8)),
            dma((2, 8)),
            dma((2, 2, 4, 2)),
            dma((2, 2, 4, 2)),
            dma((2, 9)),
            dma((2, 9)),
            dma((2, 8)),
            dma((2, 8)),
            dma((2, 3)),
            dma((2, 3)),
            dma((2, 8, NS)),
            dma((2, 8, NS)),
        ],
        compiler_params=pltpu.CompilerParams(
            collective_id=0, has_side_effects=True, vmem_limit_bytes=60 * 1024 * 1024
        ),
    )(tokens, expert_ids.T, combine_weights.T, w_gate, w_up, w_down.transpose(0, 2, 1))


def solution(mesh):
    placed = (
        P("expert", "dp"),
        P("expert", None),
        P("expert", None),
        P("expert", "dp", None),
        P("expert", "dp", None),
        P("expert", None, "dp"),
    )
    return jax.shard_map(
        shards, mesh=mesh, in_specs=placed, out_specs=P("expert", "dp"), check_vma=False
    )
```

time: 142 us -> 118 us (0.83)
  the two profiles are of different devices: /device:TPU:64 before, /device:TPU:8 now
where the time goes in v2:
time: 118 us
  Pallas kernels  117 us (99%)
  local copies, waits for them, and re-layouts  1.47 us (1%)
    pallas_call x1, Pallas kernels, shards(): pl.pallas_call(body, out_shape=jax.ShapeDtypeStruct((rows, width), BF16),...  117 us

profile of v2, /device:TPU:8, one launch (start us, length us, event | category | flops | bytes accessed | tf_op | source)
XLA Modules:
  0.0 118.1 jit_solution(5111485978475453646)
XLA Ops:
  0.0 116.6 %shard_map.64 = bf16[64,448]{1,0:T(8,128)(2,1)} custom-call(bf16[64,448]{1,0:T(8,128)(2,1)} %tok.1, s32[8,64]{1,0:T(8,128)} %bitcast.4, f32[8,64]{1,0:T(8,128)} %bitcast.5, bf16[1,448,1024]{2,1,0:T(8,128)(2,1)} %wg_hbm.1, bf16[1,448,1024]{2,1,0:T(8,128)(2,1)} %wu_hbm.1, bf16[1,448,1024]{2,1,0:T(8,128)(2,1)} %bitcast.3), custom_call_target="tpu_custom_call" | custom-call | tf_op jit(solution)/shard_map/pallas_call | solution.py:384
  116.6 1.5 %copy.8 = bf16[64,448]{1,0:T(8,128)(2,1)} copy(bf16[64,448]{1,0:T(8,128)(2,1)} %shard_map.64) | data formatting | bytes 114688

commit v3 on v2

--- a/solution.py
+++ b/solution.py
@@ -286,6 +286,23 @@
         res = res + lax.dot_general(wt_lo[g], rows, dims, preferred_element_type=F32)
         pt[8 * g : 8 * g + 8] = res.reshape(8, 64, padded)
 
+    low = lax.broadcasted_iota(jnp.int32, (half // 2, 128), 1) < 64
+
+    def pack(to, value):
+        for tile in range(3):
+            to[tile * half : (tile + 1) * half, :] = value[:, 128 * tile : 128 * tile + 128].astype(BF16)
+        rest = value[:, 384:512]
+        both = jnp.where(low, rest[: half // 2], pltpu.roll(rest[half // 2 :], 64, 1))
+        to[3 * half :, :] = both.astype(BF16)
+
+    def unpack(value):
+        value = value.astype(F32)
+        both = value[3 * half :]
+        rest = jnp.concatenate(
+            [jnp.where(low, both, 0.0), jnp.where(low, pltpu.roll(both, 64, 1), 0.0)], axis=0
+        )
+        return jnp.concatenate([value[tile * half : (tile + 1) * half] for tile in range(3)] + [rest], axis=1)
+
     zr = {}
     for way in range(2):
         for k in range(1, 9):
@@ -307,8 +324,8 @@
                 for before in (k + 1, k + 2):
                     if k % 2 == 0 and (way, before, sub) in zr:
                         zr[way, before, sub].wait_recv()
-                        value = value + rz[way, before - 1, sub].astype(F32)
-                zs[way, k - 1, sub] = value.astype(BF16)
+                        value = value + unpack(rz[way, before - 1, sub])
+                pack(zs.at[way, k - 1, sub], value)
                 zr[way, k, sub].start()
 
     def sent(*groups):
@@ -325,24 +342,24 @@
     loads[1].wait()
     for j in range(1, NX):
         xa[0, j].wait_recv()
-    parts(0, 0, 3)
+    parts(0, 0, 1)
     z_go(6)
     y_step(0, 4)
-    parts(0, 3, 5)
+    parts(0, 1, 5)
+    z_take(5, 7, 8)
+    select(1)
     y_step(0, 3)
     parts(0, 5, 8)
-    z_take(5, 7, 8)
-    select(1)
-    y_step(0, 2)
     for j in range(1, NX):
         xa[1, j].wait_recv()
-    parts(1, 0, 3)
+    parts(1, 0, 1)
+    y_step(0, 2)
     y_step(1, 4)
+    parts(1, 1, 5)
     y_step(0, 1)
-    parts(1, 3, 5)
     y_step(1, 3)
+    parts(1, 5, 8)
     activate(0)
-    parts(1, 5, 8)
     y_step(1, 2)
     gather(0, 1, 5)
     y_step(1, 1)
@@ -369,7 +386,7 @@
         for way in range(2):
             for k in (1, 2):
                 zr[way, k, sub].wait_recv()
-                total = total + rz[way, k - 1, sub].astype(F32)
+                total = total + unpack(rz[way, k - 1, sub])
         out[sub * half : (sub + 1) * half, :] = total[:, 0:width].astype(BF16)
     sent(zr.values())
 
@@ -404,8 +421,8 @@
             pltpu.VMEM((2, 4, 80, padded), BF16),
             pltpu.VMEM((2, 4, 80, padded), BF16),
             pltpu.VMEM((16, 64, padded), F32),
-            pltpu.VMEM((2, 8, NS, 64 // NS, padded), BF16),
-            pltpu.VMEM((2, 8, NS, 64 // NS, padded), BF16),
+            pltpu.VMEM((2, 8, NS, 64 // NS * 7 // 2, 128), BF16),
+            pltpu.VMEM((2, 8, NS, 64 // NS * 7 // 2, 128), BF16),
             dma((3,)),
             dma((2, 8, NS)),
             dma((2, 8, NS)),

time: 118 us -> 115 us (0.975)
  Pallas kernels: 117 us -> 113 us
    pallas_call x1, Pallas kernels: 117 us -> 113 us  [shards(): pl.pallas_call(body, out_shape=jax.ShapeDtypeStruct((rows, width), BF16),...]
where the time goes in v3:
time: 115 us; the launch traced here: 114 us
  Pallas kernels  113 us (98%)
  local copies, waits for them, and re-layouts  1.47 us (1%)
    pallas_call x1, Pallas kernels, shards(): pl.pallas_call(body, out_shape=jax.ShapeDtypeStruct((rows, width), BF16),...  113 us

profile of v3, /device:TPU:8, one launch (start us, length us, event | category | flops | bytes accessed | tf_op | source)
XLA Modules:
  0.0 114.4 jit_solution(10479970550880225662)
XLA Ops:
  0.0 112.9 %shard_map.64 = bf16[64,448]{1,0:T(8,128)(2,1)} custom-call(bf16[64,448]{1,0:T(8,128)(2,1)} %tok.1, s32[8,64]{1,0:T(8,128)} %bitcast.4, f32[8,64]{1,0:T(8,128)} %bitcast.5, bf16[1,448,1024]{2,1,0:T(8,128)(2,1)} %wg_hbm.1, bf16[1,448,1024]{2,1,0:T(8,128)(2,1)} %wu_hbm.1, bf16[1,448,1024]{2,1,0:T(8,128)(2,1)} %bitcast.3), custom_call_target="tpu_custom_call" | custom-call | tf_op jit(solution)/shard_map/pallas_call | solution.py:401
  112.9 1.5 %copy.8 = bf16[64,448]{1,0:T(8,128)(2,1)} copy(bf16[64,448]{1,0:T(8,128)(2,1)} %shard_map.64) | data formatting | bytes 114688

commit v4 on v3

--- a/solution.py
+++ b/solution.py
@@ -17,7 +17,7 @@
 
 def body(
     tok, ids, wts, wg_hbm, wu_hbm, wd_hbm, out,
-    wg, wu, wd, blk, meta, xs, xr, wt_hi, wt_lo, part, prx, sb, rr, hid, ob, yb, pt, zs, rz,
+    wg, wu, wd, blk, meta, xs, xr, wt_hi, wt_lo, part, prx, sb, rr, sb16, rr16, hid, ob, yb, pt, zs, rz,
     w_sem, za_s, za_r, zm_s, zm_r, xa_s, xa_r, pp_s, pp_r, rs_s, rs_r,
     ag_s, ag_r, ph_s, ph_r, xb_s, xb_r, zr_s, zr_r,
 ):
@@ -180,8 +180,9 @@
                 for m in range(2):
                     if k == 4 and m != way:
                         continue
+                    out_at, in_at = (sb16, rr16) if k > 2 else (sb, rr)
                     rs[g, way, k, m] = remote(
-                        sb.at[g, way, k - 1, m], rr.at[g, way, k - 1, m],
+                        out_at.at[g, way, (k - 1) % 2, m], in_at.at[g, way, (k - 1) % 2, m],
                         rs_s.at[g, way, k - 1, m], rs_r.at[g, way, k - 1, m], y_dev[way],
                     )
 
@@ -196,8 +197,11 @@
                 value = part[g, s, c, m] + prx[g, s, m]
                 if (g, way, k + 1, m) in rs:
                     rs[g, way, k + 1, m].wait_recv()
-                    value = value + rr[g, way, k, m]
-                sb[g, way, k - 1, m] = value
+                    value = value + (rr16 if k > 1 else rr)[g, way, k % 2, m].astype(F32)
+                if k > 2:
+                    sb16[g, way, (k - 1) % 2, m] = value.astype(BF16)
+                else:
+                    sb[g, way, k - 1, m] = value
                 rs[g, way, k, m].start()
 
     def unit(k):
@@ -415,8 +419,10 @@
             pltpu.VMEM((2, 320, 512), BF16),
             pltpu.VMEM((2, 8, 2, 2, 160, 128), F32),
             pltpu.VMEM((2, 8, 2, 160, 128), F32),
-            pltpu.VMEM((2, 2, 4, 2, 160, 128), F32),
-            pltpu.VMEM((2, 2, 4, 2, 160, 128), F32),
+            pltpu.VMEM((2, 2, 2, 2, 160, 128), F32),
+            pltpu.VMEM((2, 2, 2, 2, 160, 128), F32),
+            pltpu.VMEM((2, 2, 2, 2, 160, 128), BF16),
+            pltpu.VMEM((2, 2, 2, 2, 160, 128), BF16),
             pltpu.VMEM((2, 2, 8, 160, 128), BF16),
             pltpu.VMEM((2, 4, 80, padded), BF16),
             pltpu.VMEM((2, 4, 80, padded), BF16),

time: 115 us -> 114 us (level)
  no operation moved by 1% of the time
where the time goes in v4:
time: 114 us
  Pallas kernels  113 us (99%)
  local copies, waits for them, and re-layouts  1.47 us (1%)
    pallas_call x1, Pallas kernels, shards(): pl.pallas_call(body, out_shape=jax.ShapeDtypeStruct((rows, width), BF16),...  113 us

profile of v4, /device:TPU:8, one launch (start us, length us, event | category | flops | bytes accessed | tf_op | source)
XLA Modules:
  0.0 114.2 jit_solution(3821019429065688947)
XLA Ops:
  0.0 112.7 %shard_map.64 = bf16[64,448]{1,0:T(8,128)(2,1)} custom-call(bf16[64,448]{1,0:T(8,128)(2,1)} %tok.1, s32[8,64]{1,0:T(8,128)} %bitcast.4, f32[8,64]{1,0:T(8,128)} %bitcast.5, bf16[1,448,1024]{2,1,0:T(8,128)(2,1)} %wg_hbm.1, bf16[1,448,1024]{2,1,0:T(8,128)(2,1)} %wu_hbm.1, bf16[1,448,1024]{2,1,0:T(8,128)(2,1)} %bitcast.3), custom_call_target="tpu_custom_call" | custom-call | tf_op jit(solution)/shard_map/pallas_call | solution.py:405
  112.7 1.5 %copy.8 = bf16[64,448]{1,0:T(8,128)(2,1)} copy(bf16[64,448]{1,0:T(8,128)(2,1)} %shard_map.64) | data formatting | bytes 114688
